TPU v7x, 32 devices: a whole 2x2x4 slice. The times are simulated.
32 devices in a mesh: groups: 2 (over x), tile: 16 (over z, y, core).
Axes of the slice: x: 2, y: 2, z: 4, core: 2. Of those that a mesh axis runs over, the one named last changes fastest.
Arguments:
- fine_nodes: bfloat16 [32768, 512], P(('groups', 'tile')), parts along dimension 0, may hold values from -6 to 6
- fine_table: int32 [16384, 6], P('tile'), may hold values from 0 to 16383, as said below
- mid_table: int32 [4096, 6], P('tile'), may hold values from 0 to 4095, as said below
- coarse_table: int32 [1024, 6], replicated, may hold values from 0 to 1023, as said below
- fine_parent: int32 [16384], P('tile'), may hold values from 0 to 4095, as said below
- mid_parent: int32 [4096], P('tile'), may hold values from 0 to 1023, as said below
- edge_self: bfloat16 [3, 512, 512], replicated, may hold values from -0.1875 to 0.1875
- edge_peer: bfloat16 [3, 512, 512], replicated, may hold values from -0.1875 to 0.1875
- edge_bias: float32 [3, 512], replicated, may hold values from -3 to 3
- node_self: bfloat16 [3, 512, 512], replicated, may hold values from -0.1875 to 0.1875
- node_message: bfloat16 [3, 512, 512], replicated, may hold values from -0.109375 to 0.109375
- node_bias: float32 [3, 512], replicated, may hold values from -3 to 3
- node_out: bfloat16 [3, 512, 512], replicated, may hold values from -0.25 to 0.25
- ascend_gain: float32 [2, 512], replicated, may hold values from 0.1 to 1.9
- down_self: bfloat16 [2, 512, 512], replicated, may hold values from -0.1875 to 0.1875
- down_parent: bfloat16 [2, 512, 512], replicated, may hold values from -0.1875 to 0.1875
- down_bias: float32 [2, 512], replicated, may hold values from -3 to 3
- down_out: bfloat16 [2, 512, 512], replicated, may hold values from -0.25 to 0.25
Outputs:
- fine_out: bfloat16 [32768, 512], P(('groups', 'tile')), parts along dimension 0
- mid_out: bfloat16 [8192, 512], P(('groups', 'tile')), parts along dimension 0
- coarse_out: bfloat16 [2048, 512], P(('groups', 'tile')), parts along dimension 0
There are 2 independent parts, one for each index of `groups`. A program takes and returns all parts, laid end to end along the dimension named above; an argument that names none is the same for every part. Nothing has to cross between parts.
Inputs may be any that keep to these rules, and one draw needn't show every extreme that they name: `fine_table`: fine node n is grid cell (n // 256, n % 256); each of its six neighbours lies in its own grid row or one of the two rows beside it, columns wrapping around. `mid_table`: Level-1 node p is cell (p // 128, p % 128); each neighbour lies in its own row or one of the two rows beside it, columns wrapping around. `coarse_table`: any level-2 nodes. `fine_parent`: the parent of fine cell (r, c) lies in level-1 row r // 2 - 1, r // 2 or r // 2 + 1. `mid_parent`: the parent of level-1 cell (r, c) lies in level-2 row r // 2 - 1, r // 2 or r // 2 + 1.
All inputs are finite; a program needn't handle non-finite values.
Results may differ from a plain program's by a relative error of at most 0.014.
Values may be sent and summed in bfloat16 or wider, within the bound.
A program may use at most 64 MiB of HBM per device.

v0:
```python
import jax
import jax.numpy as jnp
from jax import lax
from jax.sharding import PartitionSpec as P

COLS = 256


def with_halo(cells, sides, width):
    for axis, dim in sides:
        count = lax.axis_size(axis)
        ends = count - 1
        head = lax.slice_in_dim(cells, 0, width, axis=dim)
        tail = lax.slice_in_dim(cells, cells.shape[dim] - width, cells.shape[dim], axis=dim)
        cells = jnp.concatenate(
            [
                lax.ppermute(tail, axis, [(i, (i + 1) % count) for i in range(ends)]),
                cells,
                lax.ppermute(head, axis, [((i + 1) % count, i) for i in range(ends)]),
            ],
            axis=dim,
        )
    return cells


def gelu_tanh(values):
    return jax.nn.gelu(values, approximate=True)


def rim_rows(block_rows, col_count):
    feature_count = block_rows.shape[1]
    grid_rows = block_rows.reshape(block_rows.shape[0] // col_count, col_count, feature_count)
    padded = with_halo(grid_rows, (("tile", 0),), 1)
    return padded.reshape(-1, feature_count)


def finish_level(node_rows, summed, level_index, weights):
    node_self = weights[3]
    node_message = weights[4]
    node_bias = weights[5]
    node_out = weights[6]
    message = summed.astype(jnp.bfloat16)
    pre_act = jnp.dot(node_rows, node_self[level_index], preferred_element_type=jnp.float32)
    pre_act = (
        pre_act
        + jnp.dot(message, node_message[level_index], preferred_element_type=jnp.float32)
        + node_bias[level_index]
    )
    hidden = gelu_tanh(pre_act).astype(jnp.bfloat16)
    result = node_rows.astype(jnp.float32) + jnp.dot(
        hidden, node_out[level_index], preferred_element_type=jnp.float32
    )
    return result.astype(jnp.bfloat16)


def own_projection(node_rows, level_index, weights):
    return (
        jnp.dot(node_rows, weights[0][level_index], preferred_element_type=jnp.float32)
        + weights[2][level_index]
    )


def peer_projection(node_rows, level_index, weights):
    return jnp.dot(node_rows, weights[1][level_index], preferred_element_type=jnp.float32).astype(
        jnp.bfloat16
    )


def process_local(node_rows, neighbours, level_index, col_count, weights):
    own_proj = own_projection(node_rows, level_index, weights)
    extended = rim_rows(peer_projection(node_rows, level_index, weights), col_count)
    offset = lax.axis_index("tile") * node_rows.shape[0] - col_count
    local_ids = neighbours - offset
    summed = jnp.zeros(own_proj.shape, jnp.float32)
    for slot_index in range(6):
        fetched = extended[local_ids[:, slot_index]].astype(jnp.float32)
        summed = summed + gelu_tanh(own_proj + fetched)
    return finish_level(node_rows, summed, level_index, weights)


def ascend_local(children, parents, col_up, gain_vec):
    feature_count = children.shape[1]
    rows_up = children.shape[0] // (4 * col_up)
    span_rows = (rows_up + 2) * col_up
    offset = lax.axis_index("tile") * rows_up * col_up - col_up
    local_ids = parents - offset
    onehot = (local_ids[None, :] == jnp.arange(span_rows, dtype=jnp.int32)[:, None]).astype(
        jnp.bfloat16
    )
    partial_value = jnp.dot(onehot, children, preferred_element_type=jnp.float32)
    grid_rows = partial_value.reshape(rows_up + 2, col_up, feature_count)
    padded = with_halo(grid_rows.astype(jnp.bfloat16), (("tile", 0),), 1).astype(grid_rows.dtype)
    summed = grid_rows[1:-1]
    summed = summed.at[0].add(padded[0])
    summed = summed.at[-1].add(padded[-1])
    summed = summed.reshape(rows_up * col_up, feature_count)
    scale_inv = lax.rsqrt(jnp.mean(summed * summed, axis=1, keepdims=True) + 1e-05)
    return (summed * scale_inv * gain_vec).astype(jnp.bfloat16)


def descend_local(children, lifted_ext, parents, col_up, level_index, downs):
    down_self, down_parent, down_bias, down_out = downs
    rows_up = children.shape[0] // (4 * col_up)
    offset = lax.axis_index("tile") * rows_up * col_up - col_up
    fetched = lifted_ext[parents - offset].astype(jnp.float32)
    pre_act = (
        jnp.dot(children, down_self[level_index], preferred_element_type=jnp.float32)
        + fetched
        + down_bias[level_index]
    )
    hidden = gelu_tanh(pre_act).astype(jnp.bfloat16)
    result = children.astype(jnp.float32) + jnp.dot(
        hidden, down_out[level_index], preferred_element_type=jnp.float32
    )
    return result.astype(jnp.bfloat16)


def local(
    fine_nodes,
    fine_table,
    mid_table,
    coarse_table,
    fine_parent,
    mid_parent,
    edge_self,
    edge_peer,
    edge_bias,
    node_self,
    node_message,
    node_bias,
    node_out,
    ascend_gain,
    down_self,
    down_parent,
    down_bias,
    down_out,
):
    weights = (edge_self, edge_peer, edge_bias, node_self, node_message, node_bias, node_out)
    downs = (down_self, down_parent, down_bias, down_out)
    col_mid = COLS // 2
    col_low = COLS // 4
    fine_rows = process_local(fine_nodes, fine_table, 0, COLS, weights)
    mid_start = ascend_local(fine_rows, fine_parent, col_mid, ascend_gain[0])
    mid_rows = process_local(mid_start, mid_table, 1, col_mid, weights)
    coarse_start = ascend_local(mid_rows, mid_parent, col_low, ascend_gain[1])
    coarse_count = coarse_start.shape[0]
    peer_proj = peer_projection(coarse_start, 2, weights)
    own_proj = own_projection(coarse_start, 2, weights)
    my_table = lax.dynamic_slice_in_dim(
        coarse_table, lax.axis_index("tile") * coarse_count, coarse_count, 0
    )
    running = jnp.zeros(own_proj.shape, jnp.float32)
    fragment = lax.all_gather(peer_proj, "tile", axis=0, tiled=True)
    row_count = fragment.shape[0]
    for slot_index in range(6):
        where_ids = my_table[:, slot_index]
        inside = (where_ids >= 0) & (where_ids < row_count)
        fetched = fragment[jnp.clip(where_ids, 0, row_count - 1)].astype(jnp.float32)
        running = running + jnp.where(inside[:, None], gelu_tanh(own_proj + fetched), 0.0)
    coarse_final = finish_level(coarse_start, running, 2, weights)
    lifted_own = jnp.dot(coarse_final, down_parent[1], preferred_element_type=jnp.float32).astype(
        jnp.bfloat16
    )
    lifted_ext = rim_rows(lifted_own, col_low)
    mid_final = descend_local(mid_rows, lifted_ext, mid_parent, col_low, 1, downs)
    lifted_mid = rim_rows(
        jnp.dot(mid_final, down_parent[0], preferred_element_type=jnp.float32).astype(jnp.bfloat16),
        col_mid,
    )
    fine_final = descend_local(fine_rows, lifted_mid, fine_parent, col_mid, 0, downs)
    return (fine_final, mid_final, coarse_final)


def solution(mesh):
    placed = (
        P(("groups", "tile"), None),
        P("tile", None),
        P("tile", None),
        P(),
        P("tile"),
        P("tile"),
        P(),
        P(),
        P(),
        P(),
        P(),
        P(),
        P(),
        P(),
        P(),
        P(),
        P(),
        P(),
    )
    return jax.shard_map(
        local,
        mesh=mesh,
        in_specs=placed,
        out_specs=(
            P(("groups", "tile"), None),
            P(("groups", "tile"), None),
            P(("groups", "tile"), None),
        ),
        check_vma=False,
    )
```

profile of v0, /device:TPU:5, one launch (start us, length us, event | category | flops | bytes accessed | tf_op | source)
XLA Modules:
  0.0 196.6 jit_solution(9857290049073583987)
XLA Ops:
  9.5 3.8 %collective-permute-start = (bf16[1,256,512]{2,1,0:T(8,128)(2,1)S(1)}, bf16[1,256,512]{2,1,0:T(8,128)(2,1)S(1)}, u32[]{:S(2)}, u32[]{:S(2)}) collective-permute-start(bf16[1,256,512]{2,1,0:T(8,128)(2,1)S(1)} %get-tuple-element.57), channel_id=1, source_target_pairs={{0,1},{1,2},{2,3},{3,4},{4,5},{5,6},{6,7},{7,8},{8,9},{9,10},{10,1... | collective-permute-start | bytes 786440 | tf_op jit(solution)/shard_map/ppermute | solution.py:17
  15.5 3.1 %fusion.175 = f32[1024,512]{1,0:T(8,128)} fusion(bf16[1024,512]{1,0:T(8,128)(2,1)S(1)} %copy-done.3, bf16[3,512,512]{2,1,0:T(8,128)(2,1)} %param.35), kind=kOutput, calls=%fused_computation.221 | convolution fusion | flops 536870912 | bytes 3670016 | tf_op jit(solution)/shard_map/dot_general | solution.py:43
  18.7 3.2 %collective-permute-done.1 = bf16[1,256,512]{2,1,0:T(8,128)(2,1)S(1)} collective-permute-done((bf16[1,256,512]{2,1,0:T(8,128)(2,1)S(1)}, bf16[1,256,512]{2,1,0:T(8,128)(2,1)S(1)}, u32[]{:S(2)}, u32[]{:S(2)}) %collective-permute-start.1) | collective-permute-done | bytes 262176 | tf_op jit(solution)/shard_map/ppermute | solution.py:19
  22.1 5.1 %gather_fusion = bf16[1024,512]{1,0:T(8,128)(2,1)} fusion(bf16[1536,512]{1,0:T(8,128)(2,1)S(1)} %bitcast.201, s32[1024]{0:T(1024)S(1)} %broadcast_clamp_fusion.5), kind=kCustom, calls=%fused_computation | custom fusion | bytes 2101248 | tf_op jit(solution)/shard_map/gather | solution.py:76
  27.2 5.1 %gather_fusion.1 = bf16[1024,512]{1,0:T(8,128)(2,1)} fusion(bf16[1536,512]{1,0:T(8,128)(2,1)S(1)} %bitcast.202, s32[1024]{0:T(1024)S(1)} %broadcast_clamp_fusion.4), kind=kCustom, calls=%fused_computation.1 | custom fusion | bytes 2101248 | tf_op jit(solution)/shard_map/gather | solution.py:76
  32.3 5.1 %gather_fusion.2 = bf16[1024,512]{1,0:T(8,128)(2,1)} fusion(bf16[1536,512]{1,0:T(8,128)(2,1)S(1)} %bitcast.203, s32[1024]{0:T(1024)S(1)} %broadcast_clamp_fusion.3), kind=kCustom, calls=%fused_computation.2 | custom fusion | bytes 2101248 | tf_op jit(solution)/shard_map/gather | solution.py:76
  37.4 5.0 %gather_fusion.3 = bf16[1024,512]{1,0:T(8,128)(2,1)} fusion(bf16[1536,512]{1,0:T(8,128)(2,1)S(1)} %bitcast.204, s32[1024]{0:T(1024)S(1)} %broadcast_clamp_fusion.2), kind=kCustom, calls=%fused_computation.3 | custom fusion | bytes 2101248 | tf_op jit(solution)/shard_map/gather | solution.py:76
  42.4 5.1 %gather_fusion.4 = bf16[1024,512]{1,0:T(8,128)(2,1)} fusion(bf16[1536,512]{1,0:T(8,128)(2,1)S(1)} %bitcast.205, s32[1024]{0:T(1024)S(1)} %broadcast_clamp_fusion.1), kind=kCustom, calls=%fused_computation.4 | custom fusion | bytes 2101248 | tf_op jit(solution)/shard_map/gather | solution.py:76
  47.5 5.1 %gather_fusion.5 = bf16[1024,512]{1,0:T(8,128)(2,1)} fusion(bf16[1536,512]{1,0:T(8,128)(2,1)S(1)} %bitcast.206, s32[1024]{0:T(1024)S(1)} %broadcast_clamp_fusion), kind=kCustom, calls=%fused_computation.5 | custom fusion | bytes 2101248 | tf_op jit(solution)/shard_map/gather | solution.py:76
  52.5 10.0 %fusion.54 = bf16[1024,512]{1,0:T(8,128)(2,1)S(1)} fusion(f32[1024,512]{1,0:T(8,128)} %fusion.175, f32[512]{0:T(512)S(1)} %bitcast.245, bf16[1024,512]{1,0:T(8,128)(2,1)} %gather_fusion.5, bf16[1024,512]{1,0:T(8,128)(2,1)} %gather_fusion.4, bf16[1024,512]{1,0:T(8,128)(2,1)} %gather_fusion.3, bf16[1024,512]{1,0:T(8,128)(2,1)} %gather_fusion.2, ...), kind=kOutput, calls=%fused_computation.82 | convolution fusion | flops 1114636288 | bytes 11538432 | tf_op jit(solution)/shard_map/dot_general | solution.py:46
  67.0 2.6 %collective-permute-start.3 = (bf16[1,128,512]{2,1,0:T(8,128)(2,1)S(1)}, bf16[1,128,512]{2,1,0:T(8,128)(2,1)S(1)}, u32[]{:S(2)}, u32[]{:S(2)}) collective-permute-start(bf16[1,128,512]{2,1,0:T(8,128)(2,1)S(1)} %get-tuple-element.60), channel_id=1, source_target_pairs={{1,0},{2,1},{3,2},{4,3},{5,4},{6,5},{7,6},{8,7},{9,8},{10,9},{11,1... | collective-permute-start | bytes 393224 | tf_op jit(solution)/shard_map/ppermute | solution.py:19
  69.7 4.5 %collective-permute-done.3 = bf16[1,128,512]{2,1,0:T(8,128)(2,1)S(1)} collective-permute-done((bf16[1,128,512]{2,1,0:T(8,128)(2,1)S(1)}, bf16[1,128,512]{2,1,0:T(8,128)(2,1)S(1)}, u32[]{:S(2)}, u32[]{:S(2)}) %collective-permute-start.3) | collective-permute-done | bytes 131104 | tf_op jit(solution)/shard_map/ppermute | solution.py:19
  78.3 2.4 %collective-permute-start.5 = (bf16[1,128,512]{2,1,0:T(8,128)(2,1)S(1)}, bf16[1,128,512]{2,1,0:T(8,128)(2,1)S(1)}, u32[]{:S(2)}, u32[]{:S(2)}) collective-permute-start(bf16[1,128,512]{2,1,0:T(8,128)(2,1)S(1)} %get-tuple-element.64), channel_id=1, source_target_pairs={{1,0},{2,1},{3,2},{4,3},{5,4},{6,5},{7,6},{8,7},{9,8},{10,9},{11,1... | collective-permute-start | bytes 393224 | tf_op jit(solution)/shard_map/ppermute | solution.py:19
  82.9 2.6 %collective-permute-done.5 = bf16[1,128,512]{2,1,0:T(8,128)(2,1)S(1)} collective-permute-done((bf16[1,128,512]{2,1,0:T(8,128)(2,1)S(1)}, bf16[1,128,512]{2,1,0:T(8,128)(2,1)S(1)}, u32[]{:S(2)}, u32[]{:S(2)}) %collective-permute-start.5) | collective-permute-done | bytes 131104 | tf_op jit(solution)/shard_map/ppermute | solution.py:19
  96.0 3.3 %fusion.66 = bf16[256,512]{1,0:T(8,128)(2,1)S(1)} fusion(f32[256,512]{1,0:T(8,128)S(1)} %fusion.160, bf16[3,512,512]{2,1,0:T(8,128)(2,1)} %param.38, bf16[3,512,512]{2,1,0:T(8,128)(2,1)} %param.36, bf16[256,512]{1,0:T(8,128)(2,1)} %fusion.163, f32[256,512]{1,0:T(8,128)S(1)} %convolution_add_fusion.3, bf16[256,512]{1,0:T(8,128)(2,1)} %gather_fusion.11, ...), kind=kOutput, calls=%fused_computation.103 | convolution fusion | flops 278921216 | bytes 4196352 | tf_op jit(solution)/shard_map/dot_general | solution.py:50
  101.5 2.4 %collective-permute-start.7 = (bf16[1,64,512]{2,1,0:T(8,128)(2,1)S(1)}, bf16[1,64,512]{2,1,0:T(8,128)(2,1)S(1)}, u32[]{:S(2)}, u32[]{:S(2)}) collective-permute-start(bf16[1,64,512]{2,1,0:T(8,128)(2,1)S(1)} %get-tuple-element.66), channel_id=1, source_target_pairs={{1,0},{2,1},{3,2},{4,3},{5,4},{6,5},{7,6},{8,7},{9,8},{10,9},{11,1... | collective-permute-start | bytes 196616 | tf_op jit(solution)/shard_map/ppermute | solution.py:19
  103.9 4.1 %collective-permute-done.7 = bf16[1,64,512]{2,1,0:T(8,128)(2,1)S(1)} collective-permute-done((bf16[1,64,512]{2,1,0:T(8,128)(2,1)S(1)}, bf16[1,64,512]{2,1,0:T(8,128)(2,1)S(1)}, u32[]{:S(2)}, u32[]{:S(2)}) %collective-permute-start.7) | collective-permute-done | bytes 65568 | tf_op jit(solution)/shard_map/ppermute | solution.py:19
  110.5 36.7 %all-gather.2.cloned.1.call-done = bf16[1024,512]{1,0:T(8,128)(2,1)} async-done(((bf16[64,512]{1,0:T(8,128)(2,1)}), bf16[1024,512]{1,0:T(8,128)(2,1)}) %all-gather.2.cloned.1.call-update) | async-done | bytes 1048592 | tf_op jit(solution)/shard_map/all_gather | solution.py:153
  159.1 3.4 %collective-permute-start.8 = (bf16[1,64,512]{2,1,0:T(8,128)(2,1)S(1)}, bf16[1,64,512]{2,1,0:T(8,128)(2,1)S(1)}, u32[]{:S(2)}, u32[]{:S(2)}) collective-permute-start(bf16[1,64,512]{2,1,0:T(8,128)(2,1)S(1)} %fusion.70), channel_id=1, source_target_pairs={{0,1},{1,2},{2,3},{3,4},{4,5},{5,6},{6,7},{7,8},{8,9},{9,10},{10,1... | collective-permute-start | bytes 196616 | tf_op jit(solution)/shard_map/ppermute | solution.py:17
  164.5 4.5 %collective-permute-done.9 = bf16[1,64,512]{2,1,0:T(8,128)(2,1)S(1)} collective-permute-done((bf16[1,64,512]{2,1,0:T(8,128)(2,1)S(1)}, bf16[1,64,512]{2,1,0:T(8,128)(2,1)S(1)}, u32[]{:S(2)}, u32[]{:S(2)}) %collective-permute-start.9) | collective-permute-done | bytes 65568 | tf_op jit(solution)/shard_map/ppermute | solution.py:19
  174.2 2.4 %collective-permute-start.11 = (bf16[1,128,512]{2,1,0:T(8,128)(2,1)S(1)}, bf16[1,128,512]{2,1,0:T(8,128)(2,1)S(1)}, u32[]{:S(2)}, u32[]{:S(2)}) collective-permute-start(bf16[1,128,512]{2,1,0:T(8,128)(2,1)S(1)} %get-tuple-element.62), channel_id=1, source_target_pairs={{1,0},{2,1},{3,2},{4,3},{5,4},{6,5},{7,6},{8,7},{9,8},{10,9},{11,1... | collective-permute-start | bytes 393224 | tf_op jit(solution)/shard_map/ppermute | solution.py:19
  176.6 4.8 %collective-permute-done.11 = bf16[1,128,512]{2,1,0:T(8,128)(2,1)S(1)} collective-permute-done((bf16[1,128,512]{2,1,0:T(8,128)(2,1)S(1)}, bf16[1,128,512]{2,1,0:T(8,128)(2,1)S(1)}, u32[]{:S(2)}, u32[]{:S(2)}) %collective-permute-start.11) | collective-permute-done | bytes 131104 | tf_op jit(solution)/shard_map/ppermute | solution.py:19
  181.4 4.0 %gather_fusion.19 = bf16[1024,512]{1,0:T(8,128)(2,1)S(1)} fusion(bf16[512,512]{1,0:T(8,128)(2,1)S(1)} %bitcast.213, s32[1024]{0:T(1024)S(1)} %get-tuple-element.51), kind=kCustom, calls=%fused_computation.19 | custom fusion | bytes 2101248 | tf_op jit(solution)/shard_map/gather | solution.py:105
  185.4 4.3 %add_convert_fusion = bf16[1024,512]{1,0:T(8,128)(2,1)} fusion(bf16[1024,512]{1,0:T(8,128)(2,1)} %copy-done.17, bf16[1024,512]{1,0:T(8,128)(2,1)S(1)} %gather_fusion.19, f32[512]{0:T(512)S(1)} %bitcast.244, bf16[2,512,512]{2,1,0:T(8,128)(2,1)S(1)} %copy-done.15, bf16[2,512,512]{2,1,0:T(8,128)(2,1)} %param.40), kind=kOutput, calls=%fused_computation.91 | convolution fusion | flops 1081606144 | bytes 5244928 | tf_op jit(solution)/shard_map/dot_general | solution.py:112
  (125 shorter events, 49.3 us)
Async XLA Ops:
  7.2 102.9 %copy-start = (s32[1024,6]{0,1:T(8,128)S(1)}, s32[1024,6]{0,1:T(8,128)}, u32[]{:S(2)}) copy-start(s32[1024,6]{0,1:T(8,128)} %param.29) | copy-start | bytes 73732
  7.2 8.3 %copy-start.3 = (bf16[1024,512]{1,0:T(8,128)(2,1)S(1)}, bf16[1024,512]{1,0:T(8,128)(2,1)}, u32[]{:S(2)}) copy-start(bf16[1024,512]{1,0:T(8,128)(2,1)} %param.26) | copy-start | bytes 3145732
  7.2 139.9 %all-gather.2.cloned.1.call-start = ((), (), s32[]{:S(2)}) async-start(), calls=%async_computation | async-start | bytes 1114112 | tf_op jit(solution)/shard_map/all_gather | solution.py:153
  9.4 9.1 %copy-start.12 = (f32[2,512]{1,0:T(2,128)S(1)}, f32[2,512]{1,0:T(2,128)}, u32[]{:S(2)}) copy-start(f32[2,512]{1,0:T(2,128)} %param.39) | copy-start | bytes 12292
  9.5 9.1 %copy-start.11 = (s32[1024]{0:T(1024)S(1)}, s32[1024]{0:T(1024)}, u32[]{:S(2)}) copy-start(s32[1024]{0:T(1024)} %param.30) | copy-start | bytes 12292
  9.5 9.1 %copy-start.8 = (s32[256,6]{0,1:T(8,128)S(1)}, s32[256,6]{0,1:T(8,128)}, u32[]{:S(2)}) copy-start(s32[256,6]{0,1:T(8,128)} %param.28) | copy-start | bytes 18436
  9.5 9.2 %copy-start.14 = (s32[256]{0:T(256)S(1)}, s32[256]{0:T(256)}, u32[]{:S(2)}) copy-start(s32[256]{0:T(256)} %param.31) | copy-start | bytes 3076
  9.5 9.2 %copy-start.10 = (f32[3,512]{1,0:T(4,128)S(1)}, f32[3,512]{1,0:T(4,128)}, u32[]{:S(2)}) copy-start(f32[3,512]{1,0:T(4,128)} %param.34) | copy-start | bytes 18436
  9.5 9.2 %collective-permute-start = (bf16[1,256,512]{2,1,0:T(8,128)(2,1)S(1)}, bf16[1,256,512]{2,1,0:T(8,128)(2,1)S(1)}, u32[]{:S(2)}, u32[]{:S(2)}) collective-permute-start(bf16[1,256,512]{2,1,0:T(8,128)(2,1)S(1)} %get-tuple-element.57), channel_id=1, source_target_pairs={{0,1},{1,2},{2,3},{3,4},{4,5},{5,6},{6,7},{7,8},{8,9},{9,10},{10,1... | collective-permute-start | bytes 786440 | tf_op jit(solution)/shard_map/ppermute | solution.py:17
  13.4 8.6 %collective-permute-start.1 = (bf16[1,256,512]{2,1,0:T(8,128)(2,1)S(1)}, bf16[1,256,512]{2,1,0:T(8,128)(2,1)S(1)}, u32[]{:S(2)}, u32[]{:S(2)}) collective-permute-start(bf16[1,256,512]{2,1,0:T(8,128)(2,1)S(1)} %get-tuple-element.58), channel_id=1, source_target_pairs={{1,0},{2,1},{3,2},{4,3},{5,4},{6,5},{7,6},{8,7},{9,8},{10,9},{11,1... | collective-permute-start | bytes 786440 | tf_op jit(solution)/shard_map/ppermute | solution.py:19
  65.1 4.6 %collective-permute-start.2 = (bf16[1,128,512]{2,1,0:T(8,128)(2,1)S(1)}, bf16[1,128,512]{2,1,0:T(8,128)(2,1)S(1)}, u32[]{:S(2)}, u32[]{:S(2)}) collective-permute-start(bf16[1,128,512]{2,1,0:T(8,128)(2,1)S(1)} %get-tuple-element.59), channel_id=1, source_target_pairs={{0,1},{1,2},{2,3},{3,4},{4,5},{5,6},{6,7},{7,8},{8,9},{9,10},{10,1... | collective-permute-start | bytes 393224 | tf_op jit(solution)/shard_map/ppermute | solution.py:17
  67.0 7.2 %collective-permute-start.3 = (bf16[1,128,512]{2,1,0:T(8,128)(2,1)S(1)}, bf16[1,128,512]{2,1,0:T(8,128)(2,1)S(1)}, u32[]{:S(2)}, u32[]{:S(2)}) collective-permute-start(bf16[1,128,512]{2,1,0:T(8,128)(2,1)S(1)} %get-tuple-element.60), channel_id=1, source_target_pairs={{1,0},{2,1},{3,2},{4,3},{5,4},{6,5},{7,6},{8,7},{9,8},{10,9},{11,1... | collective-permute-start | bytes 393224 | tf_op jit(solution)/shard_map/ppermute | solution.py:19
  76.4 6.5 %collective-permute-start.4 = (bf16[1,128,512]{2,1,0:T(8,128)(2,1)S(1)}, bf16[1,128,512]{2,1,0:T(8,128)(2,1)S(1)}, u32[]{:S(2)}, u32[]{:S(2)}) collective-permute-start(bf16[1,128,512]{2,1,0:T(8,128)(2,1)S(1)} %get-tuple-element.63), channel_id=1, source_target_pairs={{0,1},{1,2},{2,3},{3,4},{4,5},{5,6},{6,7},{7,8},{8,9},{9,10},{10,1... | collective-permute-start | bytes 393224 | tf_op jit(solution)/shard_map/ppermute | solution.py:17
  78.3 7.2 %collective-permute-start.5 = (bf16[1,128,512]{2,1,0:T(8,128)(2,1)S(1)}, bf16[1,128,512]{2,1,0:T(8,128)(2,1)S(1)}, u32[]{:S(2)}, u32[]{:S(2)}) collective-permute-start(bf16[1,128,512]{2,1,0:T(8,128)(2,1)S(1)} %get-tuple-element.64), channel_id=1, source_target_pairs={{1,0},{2,1},{3,2},{4,3},{5,4},{6,5},{7,6},{8,7},{9,8},{10,9},{11,1... | collective-permute-start | bytes 393224 | tf_op jit(solution)/shard_map/ppermute | solution.py:19
  99.3 11.0 %copy-start.13 = (f32[2,512]{1,0:T(2,128)S(1)}, f32[2,512]{1,0:T(2,128)}, u32[]{:S(2)}) copy-start(f32[2,512]{1,0:T(2,128)} %param.42) | copy-start | bytes 12292
  99.5 4.3 %collective-permute-start.6 = (bf16[1,64,512]{2,1,0:T(8,128)(2,1)S(1)}, bf16[1,64,512]{2,1,0:T(8,128)(2,1)S(1)}, u32[]{:S(2)}, u32[]{:S(2)}) collective-permute-start(bf16[1,64,512]{2,1,0:T(8,128)(2,1)S(1)} %get-tuple-element.65), channel_id=1, source_target_pairs={{0,1},{1,2},{2,3},{3,4},{4,5},{5,6},{6,7},{7,8},{8,9},{9,10},{10,1... | collective-permute-start | bytes 196616 | tf_op jit(solution)/shard_map/ppermute | solution.py:17
  101.5 6.5 %collective-permute-start.7 = (bf16[1,64,512]{2,1,0:T(8,128)(2,1)S(1)}, bf16[1,64,512]{2,1,0:T(8,128)(2,1)S(1)}, u32[]{:S(2)}, u32[]{:S(2)}) collective-permute-start(bf16[1,64,512]{2,1,0:T(8,128)(2,1)S(1)} %get-tuple-element.66), channel_id=1, source_target_pairs={{1,0},{2,1},{3,2},{4,3},{5,4},{6,5},{7,6},{8,7},{9,8},{10,9},{11,1... | collective-permute-start | bytes 196616 | tf_op jit(solution)/shard_map/ppermute | solution.py:19
  158.9 13.0 %copy-start.6 = (bf16[64,512]{1,0:T(8,128)(2,1)}, bf16[64,512]{1,0:T(8,128)(2,1)S(1)}, u32[]{:S(2)}) copy-start(bf16[64,512]{1,0:T(8,128)(2,1)S(1)} %fusion.69) | copy-start | bytes 196612
  158.9 11.3 %copy-start.15 = (bf16[2,512,512]{2,1,0:T(8,128)(2,1)S(1)}, bf16[2,512,512]{2,1,0:T(8,128)(2,1)}, u32[]{:S(2)}) copy-start(bf16[2,512,512]{2,1,0:T(8,128)(2,1)} %param.43) | copy-start | bytes 3145732
  159.1 5.4 %collective-permute-start.8 = (bf16[1,64,512]{2,1,0:T(8,128)(2,1)S(1)}, bf16[1,64,512]{2,1,0:T(8,128)(2,1)S(1)}, u32[]{:S(2)}, u32[]{:S(2)}) collective-permute-start(bf16[1,64,512]{2,1,0:T(8,128)(2,1)S(1)} %fusion.70), channel_id=1, source_target_pairs={{0,1},{1,2},{2,3},{3,4},{4,5},{5,6},{6,7},{7,8},{8,9},{9,10},{10,1... | collective-permute-start | bytes 196616 | tf_op jit(solution)/shard_map/ppermute | solution.py:17
  162.6 6.5 %collective-permute-start.9 = (bf16[1,64,512]{2,1,0:T(8,128)(2,1)S(1)}, bf16[1,64,512]{2,1,0:T(8,128)(2,1)S(1)}, u32[]{:S(2)}, u32[]{:S(2)}) collective-permute-start(bf16[1,64,512]{2,1,0:T(8,128)(2,1)S(1)} %fusion.70), channel_id=1, source_target_pairs={{1,0},{2,1},{3,2},{4,3},{5,4},{6,5},{7,6},{8,7},{9,8},{10,9},{11,1... | collective-permute-start | bytes 196616 | tf_op jit(solution)/shard_map/ppermute | solution.py:19
  171.9 13.5 %copy-start.16 = (bf16[256,512]{1,0:T(8,128)(2,1)}, bf16[256,512]{1,0:T(8,128)(2,1)S(1)}, u32[]{:S(2)}) copy-start(bf16[256,512]{1,0:T(8,128)(2,1)S(1)} %fusion.67) | copy-start | bytes 786436
  172.3 4.3 %collective-permute-start.10 = (bf16[1,128,512]{2,1,0:T(8,128)(2,1)S(1)}, bf16[1,128,512]{2,1,0:T(8,128)(2,1)S(1)}, u32[]{:S(2)}, u32[]{:S(2)}) collective-permute-start(bf16[1,128,512]{2,1,0:T(8,128)(2,1)S(1)} %get-tuple-element.61), channel_id=1, source_target_pairs={{0,1},{1,2},{2,3},{3,4},{4,5},{5,6},{6,7},{7,8},{8,9},{9,10},{10,1... | collective-permute-start | bytes 393224 | tf_op jit(solution)/shard_map/ppermute | solution.py:17
  174.2 7.2 %collective-permute-start.11 = (bf16[1,128,512]{2,1,0:T(8,128)(2,1)S(1)}, bf16[1,128,512]{2,1,0:T(8,128)(2,1)S(1)}, u32[]{:S(2)}, u32[]{:S(2)}) collective-permute-start(bf16[1,128,512]{2,1,0:T(8,128)(2,1)S(1)} %get-tuple-element.62), channel_id=1, source_target_pairs={{1,0},{2,1},{3,2},{4,3},{5,4},{6,5},{7,6},{8,7},{9,8},{10,9},{11,1... | collective-permute-start | bytes 393224 | tf_op jit(solution)/shard_map/ppermute | solution.py:19
  (7 other events, 38.2 us)
Sparse Core Ops, SparseCore 0:
  110.2 36.9 all-gather.1
where the time goes:
time: 198 us; the launch traced here: 197 us
  waiting for transfers between devices  60.4 us (31%)
  local copies, waits for them, and re-layouts  54.7 us (28%)
  matrix products  36.1 us (18%)
  starting transfers between devices  28.6 us (14%)
  between operations  14.9 us (8%)
    gather x12, local copies, waits for them, and re-layouts, process_local(): fetched = extended[local_ids[:, slot_index]].astype(jnp.float32)  40.9 us
    all_gather x1, waiting for transfers between devices, local(): fragment = lax.all_gather(peer_proj, 'tile', axis=0, tiled=True)  36.7 us
    ppermute x6, waiting for transfers between devices, with_halo(): lax.ppermute(head, axis, [((i + 1) % count, i) for i in range(ends)])  23.7 us
    ppermute x6, starting transfers between devices, with_halo(): lax.ppermute(tail, axis, [(i, (i + 1) % count) for i in range(ends)])  14.9 us
    ppermute x6, starting transfers between devices, with_halo(): lax.ppermute(head, axis, [((i + 1) % count, i) for i in range(ends)])  13.6 us
    dot_general x1, matrix products, finish_level(): jnp.dot(message, node_message[level_index], preferred_element_type=jnp.fl...  9.98 us
    gather x6, local copies, waits for them, and re-layouts, local(): fragment[jnp.clip(where_ids, 0, row_count - 1)].astype(jnp.float32)  8.41 us
    dot_general x3, matrix products, finish_level(): jnp.dot(hidden, node_out[level_index], preferred_element_type=jnp.float32)  6.61 us
  transfers between devices with their start and end apart: 13, of which 7 were waited for; matrix products, arithmetic and copies ran while one was open for 3% of the time, Pallas kernels for 0%

commit v1 on v0

v1 whole, which is shorter than its diff:
```python
import functools

import jax
import jax.numpy as jnp
from jax import lax
from jax.experimental import pallas as pl
from jax.experimental.pallas import tpu as pltpu
from jax.sharding import PartitionSpec as P

COLS = 256
BF = jnp.bfloat16
F32 = jnp.float32


def gelu(v):
    inner = v * (0.7978845608028654 + (0.7978845608028654 * 0.044715) * (v * v))
    half = 0.5 * v
    return half + half * jnp.tanh(inner)


def mm(a, b):
    return jnp.dot(a, b, preferred_element_type=F32)


def onehot_cols(ids, width):
    lanes = lax.broadcasted_iota(jnp.int32, (ids.shape[0], width), 1)
    return jnp.where(lanes == ids, 1.0, 0.0).astype(BF)


def onehot_rows(ids, height):
    rows = lax.broadcasted_iota(jnp.int32, (height, ids.shape[1]), 0)
    return jnp.where(rows == ids, 1.0, 0.0).astype(BF)


def sweep(
    n,
    span_y,
    cols0,
    x_hbm,
    col0_ref,
    col1_ref,
    ctab_ref,
    par0_ref,
    par1_ref,
    edge_self_hbm,
    edge_peer_hbm,
    node_self_hbm,
    node_message_hbm,
    node_out_hbm,
    down_self_hbm,
    down_parent_hbm,
    down_out_hbm,
    edge_bias_ref,
    node_bias_ref,
    gain_ref,
    down_bias_ref,
    fine_out,
    mid_out,
    coarse_out,
    x,
    edge_self,
    edge_peer,
    node_self,
    node_message,
    node_out,
    down_self,
    down_parent,
    down_out,
    ext0,
    fine,
    pre0,
    send1,
    recv1,
    ext1,
    mid,
    pre1,
    send2,
    recv2,
    gath,
    extc,
    extl,
    load_sem,
    send_sem,
    recv_sem,
    gsend_z,
    gsend_y,
    gsend_c,
    grecv,
):
    me = lax.axis_index("tile")
    n0, d = x.shape
    rows0 = n0 // cols0
    c1 = cols0 // 2
    n1 = mid.shape[0]
    n2 = coarse_out.shape[0]
    c2 = n2
    has_left = me > 0
    has_right = me < n - 1
    left = jnp.maximum(me - 1, 0)
    right = jnp.minimum(me + 1, n - 1)

    loads = {}
    slot = 0

    def load(name, src, dst):
        nonlocal slot
        cp = pltpu.make_async_copy(src, dst, load_sem.at[slot])
        cp.start()
        loads[name] = cp
        slot += 1

    load("x", x_hbm, x)
    load(("edge_peer", 0), edge_peer_hbm.at[0], edge_peer.at[0])
    load(("edge_self", 0), edge_self_hbm.at[0], edge_self.at[0])
    load(("node_self", 0), node_self_hbm.at[0], node_self.at[0])
    load(("node_message", 0), node_message_hbm.at[0], node_message.at[0])
    load(("node_out", 0), node_out_hbm.at[0], node_out.at[0])
    for lv in (1, 2):
        load(("edge_peer", lv), edge_peer_hbm.at[lv], edge_peer.at[lv])
        load(("edge_self", lv), edge_self_hbm.at[lv], edge_self.at[lv])
        load(("node_self", lv), node_self_hbm.at[lv], node_self.at[lv])
        load(("node_message", lv), node_message_hbm.at[lv], node_message.at[lv])
        load(("node_out", lv), node_out_hbm.at[lv], node_out.at[lv])
    load("down_self", down_self_hbm, down_self)
    load("down_parent", down_parent_hbm, down_parent)
    load("down_out", down_out_hbm, down_out)

    span_z = n // (2 * span_y)
    core = me % 2
    yy = (me // 2) % span_y
    zz = me // (2 * span_y)

    def tile_of(z, y, c):
        return (z * span_y + y) * 2 + c

    def zother(k):
        out = 0
        bit = 1
        while bit < span_z:
            mine = (zz // bit) % 2
            out = out + (1 - mine if k & bit else mine) * bit
            bit *= 2
        return out

    z_partners = [zother(k) for k in range(1, span_z)]
    y_other = 1 - yy if span_y == 2 else None
    c_other = 1 - core

    barrier = pltpu.get_barrier_semaphore()

    @pl.when(has_left)
    def _():
        pl.semaphore_signal(barrier, inc=1, device_id={"tile": left})

    @pl.when(has_right)
    def _():
        pl.semaphore_signal(barrier, inc=1, device_id={"tile": right})

    partners = [tile_of(z, yy, core) for z in z_partners]
    if span_y == 2:
        partners.append(tile_of(zz, y_other, core))
    partners.append(tile_of(zz, yy, c_other))
    for p in partners:
        pl.semaphore_signal(barrier, inc=1, device_id={"tile": p})

    def halo(e, low, low_dst, high, high_dst):
        to_left = pltpu.make_async_remote_copy(
            src_ref=low,
            dst_ref=low_dst,
            send_sem=send_sem.at[2 * e],
            recv_sem=recv_sem.at[2 * e + 1],
            device_id={"tile": left},
        )
        to_right = pltpu.make_async_remote_copy(
            src_ref=high,
            dst_ref=high_dst,
            send_sem=send_sem.at[2 * e + 1],
            recv_sem=recv_sem.at[2 * e],
            device_id={"tile": right},
        )
        return to_left, to_right

    def send_left(h):
        @pl.when(has_left)
        def _():
            h[0].start()

    def send_right(h):
        @pl.when(has_right)
        def _():
            h[1].start()

    def wait_left(h):
        @pl.when(has_left)
        def _():
            h[1].wait_recv()

    def wait_right(h):
        @pl.when(has_right)
        def _():
            h[0].wait_recv()

    def drain(h):
        @pl.when(has_left)
        def _():
            h[0].wait_send()

        @pl.when(has_right)
        def _():
            h[1].wait_send()

    def zero_edges(low, high):
        @pl.when(me == 0)
        def _():
            low[...] = jnp.zeros(low.shape, low.dtype)

        @pl.when(me == n - 1)
        def _():
            high[...] = jnp.zeros(high.shape, high.dtype)

    zero_edges(ext0.at[pl.ds(0, cols0)], ext0.at[pl.ds(n0 + cols0, cols0)])
    zero_edges(recv1.at[0], recv1.at[1])
    zero_edges(ext1.at[pl.ds(0, c1)], ext1.at[pl.ds(n1 + c1, c1)])
    zero_edges(recv2.at[0], recv2.at[1])
    zero_edges(extc.at[pl.ds(0, c2)], extc.at[pl.ds(n2 + c2, c2)])
    zero_edges(extl.at[pl.ds(0, c1)], extl.at[pl.ds(n1 + c1, c1)])

    loads["x"].wait()
    loads[("edge_peer", 0)].wait()

    def peer_row(r):
        at = pl.multiple_of(r * cols0, cols0)
        ext0[pl.ds(pl.multiple_of(at + cols0, cols0), cols0), :] = mm(
            x[pl.ds(at, cols0), :], edge_peer[0]
        ).astype(BF)

    peer_row(0)
    peer_row(rows0 - 1)
    pl.semaphore_wait(barrier, len(partners) + has_left.astype(jnp.int32) + has_right.astype(jnp.int32))
    h0 = halo(
        0,
        ext0.at[pl.ds(cols0, cols0)],
        ext0.at[pl.ds(n0 + cols0, cols0)],
        ext0.at[pl.ds(n0, cols0)],
        ext0.at[pl.ds(0, cols0)],
    )
    send_left(h0)
    send_right(h0)

    @pl.loop(1, rows0 - 1)
    def _(r):
        peer_row(r)

    for name in ("edge_self", "node_self", "node_message", "node_out"):
        loads[(name, 0)].wait()

    def node_part(rows, message, lv):
        pre = (
            mm(rows, node_self[lv])
            + mm(message, node_message[lv])
            + node_bias_ref[pl.ds(lv, 1), :]
        )
        hidden = gelu(pre).astype(BF)
        return (rows.astype(F32) + mm(hidden, node_out[lv])).astype(BF)

    base0 = me * n0 - cols0

    def fine_row(r):
        at = pl.multiple_of(r * cols0, cols0)
        rows = x[pl.ds(at, cols0), :]
        own = mm(rows, edge_self[0]) + edge_bias_ref[pl.ds(0, 1), :]
        ids = col0_ref[pl.ds(at, cols0), :] - (base0 + at)
        total = jnp.zeros((cols0, d), F32)
        for k in range(6):
            pick = onehot_cols(ids[:, k : k + 1], 3 * cols0)
            total = total + gelu(own + mm(pick, ext0[pl.ds(at, 3 * cols0), :]))
        fine[pl.ds(at, cols0), :] = node_part(rows, total.astype(BF), 0)

    @pl.loop(1, rows0 - 1)
    def _(r):
        fine_row(r)

    wait_left(h0)
    wait_right(h0)

    @pl.loop(0, 2)
    def _(i):
        fine_row(i * (rows0 - 1))

    half0 = n0 // 2
    q0 = par0_ref[...] - me * n1
    send1[0] = mm(onehot_rows(q0[:, :half0] + c1, c1), fine[pl.ds(0, half0), :]).astype(BF)
    send1[1] = mm(onehot_rows(q0[:, half0:] - n1, c1), fine[pl.ds(half0, half0), :]).astype(BF)
    h1 = halo(1, send1.at[0], recv1.at[1], send1.at[1], recv1.at[0])
    send_left(h1)
    send_right(h1)
    sums = mm(onehot_rows(q0, n1), fine[...])
    for name in ("edge_peer", "edge_self", "node_self", "node_message", "node_out"):
        loads[(name, 1)].wait()
    wait_left(h1)
    wait_right(h1)

    def normed(total, lv):
        scale = lax.rsqrt(jnp.mean(total * total, axis=1, keepdims=True) + 1e-05)
        return (total * scale * gain_ref[pl.ds(lv, 1), :]).astype(BF)

    first = sums[:c1] + recv1[0].astype(F32)
    last = sums[n1 - c1 :] + recv1[1].astype(F32)
    mid0 = normed(jnp.concatenate([first, last], axis=0), 0)

    ext1[pl.ds(c1, n1), :] = mm(mid0, edge_peer[1]).astype(BF)
    h2 = halo(
        2,
        ext1.at[pl.ds(c1, c1)],
        ext1.at[pl.ds(n1 + c1, c1)],
        ext1.at[pl.ds(n1, c1)],
        ext1.at[pl.ds(0, c1)],
    )
    send_left(h2)
    send_right(h2)
    own1 = mm(mid0, edge_self[1]) + edge_bias_ref[pl.ds(1, 1), :]
    ids1 = col1_ref[...] - (me * n1 - c1)
    wait_left(h2)
    wait_right(h2)
    total1 = jnp.zeros((n1, d), F32)
    for k in range(6):
        pick = onehot_cols(ids1[:, k : k + 1], n1 + 2 * c1)
        total1 = total1 + gelu(own1 + mm(pick, ext1[...]))
    mid[...] = node_part(mid0, total1.astype(BF), 1)

    q1 = par1_ref[...] - me * n2
    send2[0] = mm(onehot_rows(q1 + c2, c2), mid[...]).astype(BF)
    send2[1] = mm(onehot_rows(q1 - n2, c2), mid[...]).astype(BF)
    h3 = halo(3, send2.at[0], recv2.at[1], send2.at[1], recv2.at[0])
    send_left(h3)
    send_right(h3)
    sums2 = mm(onehot_rows(q1, n2), mid[...])
    for name in ("edge_peer", "edge_self", "node_self", "node_message", "node_out"):
        loads[(name, 2)].wait()
    wait_left(h3)
    wait_right(h3)
    coarse0 = normed(sums2 + recv2[0].astype(F32) + recv2[1].astype(F32), 1)

    def block(t):
        return gath.at[pl.ds(pl.multiple_of(t * n2, n2), n2)]

    gath[pl.ds(pl.multiple_of(me * n2, n2), n2), :] = mm(coarse0, edge_peer[2]).astype(BF)

    def forward(t, sem, to):
        return pltpu.make_async_remote_copy(
            src_ref=block(t),
            dst_ref=block(t),
            send_sem=sem,
            recv_sem=grecv.at[t],
            device_id={"tile": to},
        )

    started = []

    def go(t, sem, to):
        cp = forward(t, sem, to)
        cp.start()
        started.append(cp)

    mate_c = tile_of(zz, yy, c_other)
    for i, z in enumerate(z_partners):
        go(me, gsend_z.at[i], tile_of(z, yy, core))
    if span_y == 2:
        go(me, gsend_y.at[0], tile_of(zz, y_other, core))
    go(me, gsend_c.at[0], mate_c)

    for name in ("down_self", "down_parent", "down_out"):
        loads[name].wait()
    own2 = mm(coarse0, edge_self[2]) + edge_bias_ref[pl.ds(2, 1), :]

    def arrived(t):
        forward(t, gsend_c.at[0], mate_c).wait_recv()

    cslot = 1
    for i, z in enumerate(z_partners):
        t = tile_of(z, yy, core)
        arrived(t)
        if span_y == 2:
            go(t, gsend_y.at[i + 1], tile_of(zz, y_other, core))
        go(t, gsend_c.at[cslot], mate_c)
        cslot += 1

    if span_y == 2:
        for z in [zz] + z_partners:
            t = tile_of(z, y_other, core)
            arrived(t)
            go(t, gsend_c.at[cslot], mate_c)
            cslot += 1

    pre1[...] = mm(mid[...], down_self[1]) + down_bias_ref[pl.ds(1, 1), :]

    @pl.loop(0, rows0)
    def _(r):
        at = pl.multiple_of(r * cols0, cols0)
        pre0[pl.ds(at, cols0), :] = (
            mm(fine[pl.ds(at, cols0), :], down_self[0]) + down_bias_ref[pl.ds(0, 1), :]
        )

    ctab = ctab_ref[pl.ds(pl.multiple_of(me * n2, n2), n2), :]
    pick2 = jnp.concatenate(
        [onehot_cols(ctab[:, k : k + 1], gath.shape[0]) for k in range(6)], axis=0
    )
    for z in [zz] + z_partners:
        for y in [yy] + ([y_other] if span_y == 2 else []):
            arrived(tile_of(z, y, c_other))
    got = mm(pick2, gath[...])
    total2 = jnp.zeros((n2, d), F32)
    for k in range(6):
        total2 = total2 + gelu(own2 + got[k * n2 : (k + 1) * n2])
    coarse = node_part(coarse0, total2.astype(BF), 2)
    coarse_out[...] = coarse

    extc[pl.ds(c2, n2), :] = mm(coarse, down_parent[1]).astype(BF)
    h4 = halo(
        4,
        extc.at[pl.ds(c2, c2)],
        extc.at[pl.ds(n2 + c2, c2)],
        extc.at[pl.ds(n2, c2)],
        extc.at[pl.ds(0, c2)],
    )
    send_left(h4)
    send_right(h4)
    pick1 = onehot_cols(col1_ref[:, 6:7] - (me * n2 - c2), n2 + 2 * c2)
    wait_left(h4)
    wait_right(h4)
    hidden1 = gelu(pre1[...] + mm(pick1, extc[...])).astype(BF)
    mid_last = (mid[...].astype(F32) + mm(hidden1, down_out[1])).astype(BF)
    mid_out[...] = mid_last

    extl[pl.ds(c1, n1), :] = mm(mid_last, down_parent[0]).astype(BF)
    h5 = halo(
        5,
        extl.at[pl.ds(c1, c1)],
        extl.at[pl.ds(n1 + c1, c1)],
        extl.at[pl.ds(n1, c1)],
        extl.at[pl.ds(0, c1)],
    )
    send_left(h5)
    send_right(h5)
    wait_left(h5)
    wait_right(h5)

    @pl.loop(0, rows0)
    def _(r):
        at = pl.multiple_of(r * cols0, cols0)
        low = pl.multiple_of((r // 2) * c1, c1)
        pick = onehot_cols(col0_ref[pl.ds(at, cols0), 6:7] - (me * n1 - c1 + low), 3 * c1)
        lifted = mm(pick, extl[pl.ds(low, 3 * c1), :])
        hidden = gelu(pre0[pl.ds(at, cols0), :] + lifted).astype(BF)
        fine_out[pl.ds(at, cols0), :] = (
            fine[pl.ds(at, cols0), :].astype(F32) + mm(hidden, down_out[0])
        ).astype(BF)

    for h in (h0, h1, h2, h3, h4, h5):
        drain(h)
    for cp in started:
        cp.wait_send()


def local(
    n,
    span_y,
    fine_nodes,
    fine_table,
    mid_table,
    coarse_table,
    fine_parent,
    mid_parent,
    edge_self,
    edge_peer,
    edge_bias,
    node_self,
    node_message,
    node_bias,
    node_out,
    ascend_gain,
    down_self,
    down_parent,
    down_bias,
    down_out,
):
    n0, d = fine_nodes.shape
    n1 = mid_table.shape[0]
    n2 = coarse_table.shape[0] // n
    c1 = COLS // 2
    c2 = n2
    span_z = n // (2 * span_y)
    col0 = jnp.concatenate([fine_table, fine_parent[:, None]], axis=1)
    col1 = jnp.concatenate([mid_table, mid_parent[:, None]], axis=1)
    vm = pl.BlockSpec(memory_space=pltpu.VMEM)
    hbm = pl.BlockSpec(memory_space=pl.ANY)
    dma = pltpu.SemaphoreType.DMA
    return pl.pallas_call(
        functools.partial(sweep, n, span_y, COLS),
        out_shape=(
            jax.ShapeDtypeStruct((n0, d), BF),
            jax.ShapeDtypeStruct((n1, d), BF),
            jax.ShapeDtypeStruct((n2, d), BF),
        ),
        in_specs=[hbm] + [vm] * 5 + [hbm] * 8 + [vm] * 4,
        out_specs=(vm, vm, vm),
        scratch_shapes=[
            pltpu.VMEM((n0, d), BF),
            *[pltpu.VMEM((3, d, d), BF)] * 5,
            *[pltpu.VMEM((2, d, d), BF)] * 3,
            pltpu.VMEM((n0 + 2 * COLS, d), BF),
            pltpu.VMEM((n0, d), BF),
            pltpu.VMEM((n0, d), F32),
            pltpu.VMEM((2, c1, d), BF),
            pltpu.VMEM((2, c1, d), BF),
            pltpu.VMEM((n1 + 2 * c1, d), BF),
            pltpu.VMEM((n1, d), BF),
            pltpu.VMEM((n1, d), F32),
            pltpu.VMEM((2, c2, d), BF),
            pltpu.VMEM((2, c2, d), BF),
            pltpu.VMEM((n * n2, d), BF),
            pltpu.VMEM((n2 + 2 * c2, d), BF),
            pltpu.VMEM((n1 + 2 * c1, d), BF),
            dma((19,)),
            dma((12,)),
            dma((12,)),
            dma((max(span_z - 1, 1),)),
            dma((span_z,)),
            dma((n // 2,)),
            dma((n,)),
        ],
        compiler_params=pltpu.CompilerParams(
            collective_id=0, has_side_effects=True, vmem_limit_bytes=60 * 1024 * 1024
        ),
        name="sweep",
    )(
        fine_nodes,
        col0,
        col1,
        coarse_table,
        fine_parent[None, :],
        mid_parent[None, :],
        edge_self,
        edge_peer,
        node_self,
        node_message,
        node_out,
        down_self,
        down_parent,
        down_out,
        edge_bias,
        node_bias,
        ascend_gain,
        down_bias,
    )


def solution(mesh):
    n = mesh.shape["tile"]
    span_y = 2 if mesh.shape["groups"] == 2 else 1
    rep = P()
    return jax.shard_map(
        functools.partial(local, n, span_y),
        mesh=mesh,
        in_specs=(P(("groups", "tile"), None), P("tile", None), P("tile", None), rep, P("tile"), P("tile"))
        + (rep,) * 12,
        out_specs=(P(("groups", "tile"), None),) * 3,
        check_vma=False,
    )
```

time: 198 us -> 68.1 us (0.34)
  waiting for transfers between devices: 60.4 us -> 0 us
  Pallas kernels: 0 us -> 58.3 us
  local copies, waits for them, and re-layouts: 54.7 us -> 7.25 us
  matrix products: 36.1 us -> 0 us
  starting transfers between devices: 28.6 us -> 0 us
  between operations: 14.9 us -> 0.66 us
    pallas_call x0 -> x1, Pallas kernels: none -> 58.3 us  [local(): pl.pallas_call(functools.partial(sweep, n, span_y, COLS), out_shape=(jax....]
    gather x20 -> x0, local copies, waits for them, and re-layouts: 54.4 us -> none  [the longest x12 40.9 us: process_local(): fetched = extended[local_ids[:, slot_index]].astype(jnp.float32)]
    all_gather x1 -> x0, waiting for transfers between devices: 36.7 us -> none  [local(): fragment = lax.all_gather(peer_proj, 'tile', axis=0, tiled=True)]
    dot_general x18 -> x0, matrix products: 36.1 us -> none  [the longest x1 9.98 us: finish_level(): jnp.dot(message, node_message[level_index], preferred_element_type=jnp.fl...]
    ppermute x12 -> x0, starting transfers between devices: 28.6 us -> none  [the longest x6 14.9 us: with_halo(): lax.ppermute(tail, axis, [(i, (i + 1) % count) for i in range(ends)])]
    ppermute x12 -> x0, waiting for transfers between devices: 23.7 us -> none  [the longest x6 23.7 us: with_halo(): lax.ppermute(head, axis, [((i + 1) % count, i) for i in range(ends)])]
    unnamed x36 -> x8, local copies, waits for them, and re-layouts: 0.11 us -> 5.43 us
  transfers between devices with their start and end apart: 13 -> 0, of which waited for: 7 -> 0; matrix products, arithmetic and copies ran while one was open for 3% -> 0% of each run, Pallas kernels for 0% -> 0%
where the time goes in v1:
time: 68.1 us; the launch traced here: 67.7 us
  Pallas kernels  58.3 us (86%)
  local copies, waits for them, and re-layouts  7.25 us (11%)
  other arithmetic  1.51 us (2%)
    pallas_call x1, Pallas kernels, local(): pl.pallas_call(functools.partial(sweep, n, span_y, COLS), out_shape=(jax....  58.3 us
    unnamed x8, local copies, waits for them, and re-layouts  5.43 us

profile of v1, /device:TPU:5, one launch (start us, length us, event | category | flops | bytes accessed | tf_op | source)
XLA Modules:
  0.0 67.7 jit_solution(12795007499193683912)
XLA Ops:
  0.6 0.7 %pad_add_fusion.1 = s32[256,7]{0,1:T(8,128)S(1)} fusion(s32[256,1]{0,1:T(1,128)} %bitcast.6, s32[256,6]{0,1:T(8,128)} %param.20), kind=kLoop, calls=%fused_computation.1 | loop fusion | flops 1792 | bytes 14336 | tf_op jit(solution)/shard_map/concatenate | solution.py:494
  1.4 0.8 %pad_add_fusion = s32[1024,7]{0,1:T(8,128)S(1)} fusion(s32[1024,1]{0,1:T(1,128)} %bitcast.4, s32[1024,6]{0,1:T(8,128)} %param.19), kind=kLoop, calls=%fused_computation | loop fusion | flops 7168 | bytes 57344 | tf_op jit(solution)/shard_map/concatenate | solution.py:493
  2.1 0.8 %copy.30.col1_ref = s32[256,7]{1,0:T(8,128)} copy(s32[256,7]{0,1:T(8,128)S(1)} %pad_add_fusion.1) | data formatting | bytes 14336 | tf_op jit(solution)/shard_map/concatenate | solution.py:494
  2.9 1.0 %copy.29.col0_ref = s32[1024,7]{1,0:T(8,128)} copy(s32[1024,7]{0,1:T(8,128)S(1)} %pad_add_fusion) | data formatting | bytes 57344 | tf_op jit(solution)/shard_map/concatenate | solution.py:493
  4.0 1.8 %copy.31.ctab_ref = s32[1024,6]{1,0:T(8,128)} copy(s32[1024,6]{0,1:T(8,128)} %param.21) | data formatting | bytes 49152 | tf_op args[3]
  5.7 58.3 %sweep.1 = (bf16[1024,512]{1,0:T(8,128)(2,1)}, bf16[256,512]{1,0:T(8,128)(2,1)}, bf16[64,512]{1,0:T(8,128)(2,1)}) custom-call(bf16[1024,512]{1,0:T(8,128)(2,1)} %x_hbm.1, s32[1024,7]{1,0:T(8,128)} %copy.29.col0_ref, s32[256,7]{1,0:T(8,128)} %copy.30.col1_ref, s32[1024,6]{1,0:T(8,128)} %copy.31.ctab_ref, s32[1,1024]{1,0:T(1,128)} %bitcast.5, ...), custom_call_target="tpu_custom_call" | custom-call | tf_op jit(solution)/shard_map/sweep/pallas_call | solution.py:498
  64.0 0.0 copy-start
  64.0 0.0 copy-start.1
  64.0 2.3 %copy.35 = bf16[1024,512]{1,0:T(8,128)(2,1)} copy(bf16[1024,512]{1,0:T(8,128)(2,1)} %get-tuple-element.6) | data formatting | bytes 2097152
  66.3 0.0 copy-done
  66.3 0.7 %copy.36 = bf16[256,512]{1,0:T(8,128)(2,1)} copy(bf16[256,512]{1,0:T(8,128)(2,1)S(1)} %copy-done) | data formatting | bytes 524288
  67.0 0.0 copy-done.1
  67.1 0.6 copy.37
Async XLA Ops:
  64.0 2.3 %copy-start = (bf16[256,512]{1,0:T(8,128)(2,1)S(1)}, bf16[256,512]{1,0:T(8,128)(2,1)}, u32[]{:S(2)}) copy-start(bf16[256,512]{1,0:T(8,128)(2,1)} %get-tuple-element.7) | copy-start | bytes 786436
  64.0 3.0 %copy-start.1 = (bf16[64,512]{1,0:T(8,128)(2,1)S(1)}, bf16[64,512]{1,0:T(8,128)(2,1)}, u32[]{:S(2)}) copy-start(bf16[64,512]{1,0:T(8,128)(2,1)} %get-tuple-element.8) | copy-start | bytes 196612

commit v2 on v1

--- a/solution.py
+++ b/solution.py
@@ -8,6 +8,8 @@
 from jax.sharding import PartitionSpec as P
 
 COLS = 256
+STACK = 3
+VMEM_MIB = 63
 BF = jnp.bfloat16
 F32 = jnp.float32
 
@@ -37,8 +39,8 @@
     span_y,
     cols0,
     x_hbm,
-    col0_ref,
-    col1_ref,
+    tab0_ref,
+    tab1_ref,
     ctab_ref,
     par0_ref,
     par1_ref,
@@ -74,11 +76,18 @@
     ext1,
     mid,
     pre1,
+    sums1,
+    mid0,
+    own1,
+    pick2,
     send2,
     recv2,
     gath,
     extc,
     extl,
+    col0_ref,
+    col1_ref,
+    ccol_ref,
     load_sem,
     send_sem,
     recv_sem,
@@ -200,6 +209,44 @@
         def _():
             h[0].wait_recv()
 
+    left_far = core == 0
+
+    def send_far(h):
+        @pl.when(has_left & left_far)
+        def _():
+            h[0].start()
+
+        @pl.when(has_right & (core == 1))
+        def _():
+            h[1].start()
+
+    def send_near(h):
+        @pl.when(has_left & (core == 1))
+        def _():
+            h[0].start()
+
+        @pl.when(has_right & left_far)
+        def _():
+            h[1].start()
+
+    def wait_far(h):
+        @pl.when(has_left & left_far)
+        def _():
+            h[1].wait_recv()
+
+        @pl.when(has_right & (core == 1))
+        def _():
+            h[0].wait_recv()
+
+    def wait_near(h):
+        @pl.when(has_left & (core == 1))
+        def _():
+            h[1].wait_recv()
+
+        @pl.when(has_right & left_far)
+        def _():
+            h[0].wait_recv()
+
     def drain(h):
         @pl.when(has_left)
         def _():
@@ -224,6 +271,15 @@
     zero_edges(recv2.at[0], recv2.at[1])
     zero_edges(extc.at[pl.ds(0, c2)], extc.at[pl.ds(n2 + c2, c2)])
     zero_edges(extl.at[pl.ds(0, c1)], extl.at[pl.ds(n1 + c1, c1)])
+
+    def columns(tab_ref, par_ref, to):
+        pad = jnp.zeros((1, tab_ref.shape[1]), jnp.int32)
+        seventh = pad if par_ref is None else par_ref[...]
+        to[...] = jnp.transpose(jnp.concatenate([tab_ref[...], seventh, pad], axis=0))
+
+    columns(tab0_ref, par0_ref, col0_ref)
+    columns(tab1_ref, par1_ref, col1_ref)
+    columns(ctab_ref, None, ccol_ref)
 
     loads["x"].wait()
     loads[("edge_peer", 0)].wait()
@@ -271,44 +327,49 @@
         own = mm(rows, edge_self[0]) + edge_bias_ref[pl.ds(0, 1), :]
         ids = col0_ref[pl.ds(at, cols0), :] - (base0 + at)
         total = jnp.zeros((cols0, d), F32)
-        for k in range(6):
-            pick = onehot_cols(ids[:, k : k + 1], 3 * cols0)
-            total = total + gelu(own + mm(pick, ext0[pl.ds(at, 3 * cols0), :]))
+        for k in range(0, 6, STACK):
+            picks = [onehot_cols(ids[:, k + j : k + j + 1], 3 * cols0) for j in range(STACK)]
+            got = mm(jnp.concatenate(picks, axis=0), ext0[pl.ds(at, 3 * cols0), :])
+            for j in range(STACK):
+                total = total + gelu(own + got[j * cols0 : (j + 1) * cols0])
         fine[pl.ds(at, cols0), :] = node_part(rows, total.astype(BF), 0)
 
     @pl.loop(1, rows0 - 1)
     def _(r):
         fine_row(r)
 
+    half0 = n0 // 2
     wait_left(h0)
     wait_right(h0)
+    h1 = halo(1, send1.at[0], recv1.at[1], send1.at[1], recv1.at[0])
+
+    def edge(side):
+        fine_row(side * (rows0 - 1))
+        at = pl.multiple_of(side * half0, half0)
+        q = par0_ref[:, pl.ds(at, half0)] - (me * n1 - c1 + side * (n1 + c1))
+        send1[side] = mm(onehot_rows(q, c1), fine[pl.ds(at, half0), :]).astype(BF)
 
     @pl.loop(0, 2)
     def _(i):
-        fine_row(i * (rows0 - 1))
-
-    half0 = n0 // 2
-    q0 = par0_ref[...] - me * n1
-    send1[0] = mm(onehot_rows(q0[:, :half0] + c1, c1), fine[pl.ds(0, half0), :]).astype(BF)
-    send1[1] = mm(onehot_rows(q0[:, half0:] - n1, c1), fine[pl.ds(half0, half0), :]).astype(BF)
-    h1 = halo(1, send1.at[0], recv1.at[1], send1.at[1], recv1.at[0])
-    send_left(h1)
-    send_right(h1)
-    sums = mm(onehot_rows(q0, n1), fine[...])
+        far = i == 0
+        edge((1 - i) * core + i * (1 - core))
+
+        @pl.when(far)
+        def _():
+            send_far(h1)
+
+        @pl.when(i == 1)
+        def _():
+            send_near(h1)
+
+    sums1[...] = mm(onehot_rows(par0_ref[...] - me * n1, n1), fine[...])
     for name in ("edge_peer", "edge_self", "node_self", "node_message", "node_out"):
         loads[(name, 1)].wait()
-    wait_left(h1)
-    wait_right(h1)
 
     def normed(total, lv):
         scale = lax.rsqrt(jnp.mean(total * total, axis=1, keepdims=True) + 1e-05)
         return (total * scale * gain_ref[pl.ds(lv, 1), :]).astype(BF)
 
-    first = sums[:c1] + recv1[0].astype(F32)
-    last = sums[n1 - c1 :] + recv1[1].astype(F32)
-    mid0 = normed(jnp.concatenate([first, last], axis=0), 0)
-
-    ext1[pl.ds(c1, n1), :] = mm(mid0, edge_peer[1]).astype(BF)
     h2 = halo(
         2,
         ext1.at[pl.ds(c1, c1)],
@@ -316,17 +377,44 @@
         ext1.at[pl.ds(n1, c1)],
         ext1.at[pl.ds(0, c1)],
     )
-    send_left(h2)
-    send_right(h2)
-    own1 = mm(mid0, edge_self[1]) + edge_bias_ref[pl.ds(1, 1), :]
-    ids1 = col1_ref[...] - (me * n1 - c1)
-    wait_left(h2)
-    wait_right(h2)
-    total1 = jnp.zeros((n1, d), F32)
-    for k in range(6):
-        pick = onehot_cols(ids1[:, k : k + 1], n1 + 2 * c1)
-        total1 = total1 + gelu(own1 + mm(pick, ext1[...]))
-    mid[...] = node_part(mid0, total1.astype(BF), 1)
+
+    def mid_start(side):
+        at = pl.multiple_of(side * c1, c1)
+        rows = normed(sums1[pl.ds(at, c1), :] + recv1[side].astype(F32), 0)
+        mid0[pl.ds(at, c1), :] = rows
+        ext1[pl.ds(pl.multiple_of(at + c1, c1), c1), :] = mm(rows, edge_peer[1]).astype(BF)
+
+    wait_near(h1)
+    mid_start(1 - core)
+    send_near(h2)
+    wait_far(h1)
+    mid_start(core)
+    send_far(h2)
+    own1[...] = mm(mid0[...], edge_self[1]) + edge_bias_ref[pl.ds(1, 1), :]
+
+    def mid_row(side):
+        at = pl.multiple_of(side * c1, c1)
+        rows = mid0[pl.ds(at, c1), :]
+        own = own1[pl.ds(at, c1), :]
+        ids = col1_ref[pl.ds(at, c1), :] - (me * n1 - c1 + at)
+        picks = jnp.concatenate([onehot_cols(ids[:, k : k + 1], 3 * c1) for k in range(6)], axis=0)
+        got = mm(picks, ext1[pl.ds(at, 3 * c1), :])
+        total = jnp.zeros((c1, d), F32)
+        for k in range(6):
+            total = total + gelu(own + got[k * c1 : (k + 1) * c1])
+        mid[pl.ds(at, c1), :] = node_part(rows, total.astype(BF), 1)
+
+    @pl.loop(0, 2)
+    def _(i):
+        @pl.when(i == 0)
+        def _():
+            wait_near(h2)
+
+        @pl.when(i == 1)
+        def _():
+            wait_far(h2)
+
+        mid_row((1 - i) * (1 - core) + i * core)
 
     q1 = par1_ref[...] - me * n2
     send2[0] = mm(onehot_rows(q1 + c2, c2), mid[...]).astype(BF)
@@ -376,6 +464,22 @@
     def arrived(t):
         forward(t, gsend_c.at[0], mate_c).wait_recv()
 
+    def pre_row(r):
+        at = pl.multiple_of(r * cols0, cols0)
+        pre0[pl.ds(at, cols0), :] = (
+            mm(fine[pl.ds(at, cols0), :], down_self[0]) + down_bias_ref[pl.ds(0, 1), :]
+        )
+
+    def pre_mid(_):
+        pre1[...] = mm(mid[...], down_self[1]) + down_bias_ref[pl.ds(1, 1), :]
+
+    work = [functools.partial(pre_row, r) for r in range(rows0)]
+    work.append(functools.partial(pre_mid, 0))
+
+    ctab = ccol_ref[pl.ds(pl.multiple_of(me * n2, n2), n2), :]
+    for k in range(6):
+        pick2[pl.ds(k * n2, n2), :] = onehot_cols(ctab[:, k : k + 1], gath.shape[0])
+
     cslot = 1
     for i, z in enumerate(z_partners):
         t = tile_of(z, yy, core)
@@ -384,6 +488,8 @@
             go(t, gsend_y.at[i + 1], tile_of(zz, y_other, core))
         go(t, gsend_c.at[cslot], mate_c)
         cslot += 1
+        if work:
+            work.pop(0)()
 
     if span_y == 2:
         for z in [zz] + z_partners:
@@ -391,24 +497,15 @@
             arrived(t)
             go(t, gsend_c.at[cslot], mate_c)
             cslot += 1
-
-    pre1[...] = mm(mid[...], down_self[1]) + down_bias_ref[pl.ds(1, 1), :]
-
-    @pl.loop(0, rows0)
-    def _(r):
-        at = pl.multiple_of(r * cols0, cols0)
-        pre0[pl.ds(at, cols0), :] = (
-            mm(fine[pl.ds(at, cols0), :], down_self[0]) + down_bias_ref[pl.ds(0, 1), :]
-        )
-
-    ctab = ctab_ref[pl.ds(pl.multiple_of(me * n2, n2), n2), :]
-    pick2 = jnp.concatenate(
-        [onehot_cols(ctab[:, k : k + 1], gath.shape[0]) for k in range(6)], axis=0
-    )
+            if work:
+                work.pop(0)()
+    for job in work:
+        job()
+
     for z in [zz] + z_partners:
         for y in [yy] + ([y_other] if span_y == 2 else []):
             arrived(tile_of(z, y, c_other))
-    got = mm(pick2, gath[...])
+    got = mm(pick2[...], gath[...])
     total2 = jnp.zeros((n2, d), F32)
     for k in range(6):
         total2 = total2 + gelu(own2 + got[k * n2 : (k + 1) * n2])
@@ -440,13 +537,10 @@
         extl.at[pl.ds(n1, c1)],
         extl.at[pl.ds(0, c1)],
     )
-    send_left(h5)
-    send_right(h5)
-    wait_left(h5)
-    wait_right(h5)
-
-    @pl.loop(0, rows0)
-    def _(r):
+    send_far(h5)
+    send_near(h5)
+
+    def last_row(r):
         at = pl.multiple_of(r * cols0, cols0)
         low = pl.multiple_of((r // 2) * c1, c1)
         pick = onehot_cols(col0_ref[pl.ds(at, cols0), 6:7] - (me * n1 - c1 + low), 3 * c1)
@@ -455,6 +549,20 @@
         fine_out[pl.ds(at, cols0), :] = (
             fine[pl.ds(at, cols0), :].astype(F32) + mm(hidden, down_out[0])
         ).astype(BF)
+
+    @pl.loop(0, rows0)
+    def _(i):
+        @pl.when(i == 0)
+        def _():
+            wait_near(h5)
+
+        @pl.when(i == rows0 // 2)
+        def _():
+            wait_far(h5)
+
+        later = i // (rows0 // 2)
+        side = (1 - later) * (1 - core) + later * core
+        last_row(i % (rows0 // 2) + side * (rows0 // 2))
 
     for h in (h0, h1, h2, h3, h4, h5):
         drain(h)
@@ -490,10 +598,8 @@
     c1 = COLS // 2
     c2 = n2
     span_z = n // (2 * span_y)
-    col0 = jnp.concatenate([fine_table, fine_parent[:, None]], axis=1)
-    col1 = jnp.concatenate([mid_table, mid_parent[:, None]], axis=1)
     vm = pl.BlockSpec(memory_space=pltpu.VMEM)
-    hbm = pl.BlockSpec(memory_space=pl.ANY)
+    hbm = pl.BlockSpec(memory_space=pltpu.HBM)
     dma = pltpu.SemaphoreType.DMA
     return pl.pallas_call(
         functools.partial(sweep, n, span_y, COLS),
@@ -516,12 +622,19 @@
             pltpu.VMEM((n1 + 2 * c1, d), BF),
             pltpu.VMEM((n1, d), BF),
             pltpu.VMEM((n1, d), F32),
+            pltpu.VMEM((n1, d), F32),
+            pltpu.VMEM((n1, d), BF),
+            pltpu.VMEM((n1, d), F32),
+            pltpu.VMEM((6 * n2, n * n2), BF),
             pltpu.VMEM((2, c2, d), BF),
             pltpu.VMEM((2, c2, d), BF),
             pltpu.VMEM((n * n2, d), BF),
             pltpu.VMEM((n2 + 2 * c2, d), BF),
             pltpu.VMEM((n1 + 2 * c1, d), BF),
-            dma((19,)),
+            pltpu.VMEM((n0, 8), jnp.int32),
+            pltpu.VMEM((n1, 8), jnp.int32),
+            pltpu.VMEM((n * n2, 8), jnp.int32),
+            dma((21,)),
             dma((12,)),
             dma((12,)),
             dma((max(span_z - 1, 1),)),
@@ -530,14 +643,14 @@
             dma((n,)),
         ],
         compiler_params=pltpu.CompilerParams(
-            collective_id=0, has_side_effects=True, vmem_limit_bytes=60 * 1024 * 1024
+            collective_id=0, has_side_effects=True, vmem_limit_bytes=VMEM_MIB * 1024 * 1024
         ),
         name="sweep",
     )(
         fine_nodes,
-        col0,
-        col1,
-        coarse_table,
+        fine_table.T,
+        mid_table.T,
+        coarse_table.T,
         fine_parent[None, :],
         mid_parent[None, :],
         edge_self,

time: 68.1 us -> 58.9 us (0.86)
  Pallas kernels: 58.3 us -> 54.4 us
  local copies, waits for them, and re-layouts: 7.25 us -> 3.65 us
  other arithmetic: 1.51 us -> 0 us
    pallas_call x1, Pallas kernels: 58.3 us -> 54.4 us  [local(): pl.pallas_call(functools.partial(sweep, n, span_y, COLS), out_shape=(jax....]
    concatenate x2 -> x0, local copies, waits for them, and re-layouts: 1.83 us -> none  [the longest x1 1.02 us: local(): col0 = jnp.concatenate([fine_table, fine_parent[:, None]], axis=1)]
    unnamed x8 -> x7, local copies, waits for them, and re-layouts: 5.43 us -> 3.65 us
    concatenate x2 -> x0, other arithmetic: 1.51 us -> none  [the longest x1 0.78 us: local(): col0 = jnp.concatenate([fine_table, fine_parent[:, None]], axis=1)]
where the time goes in v2:
time: 58.9 us; the launch traced here: 58.7 us
  Pallas kernels  54.4 us (92%)
  local copies, waits for them, and re-layouts  3.65 us (6%)
  between operations  0.66 us (1%)
    pallas_call x1, Pallas kernels, local(): pl.pallas_call(functools.partial(sweep, n, span_y, COLS), out_shape=(jax....  54.4 us
    unnamed x7, local copies, waits for them, and re-layouts  3.65 us

profile of v2, /device:TPU:5, one launch (start us, length us, event | category | flops | bytes accessed | tf_op | source)
XLA Modules:
  0.0 58.7 jit_solution(9996547190173332798)
XLA Ops:
  0.6 54.4 %sweep.1 = (bf16[1024,512]{1,0:T(8,128)(2,1)}, bf16[256,512]{1,0:T(8,128)(2,1)}, bf16[64,512]{1,0:T(8,128)(2,1)}) custom-call(bf16[1024,512]{1,0:T(8,128)(2,1)} %x_hbm.1, s32[6,1024]{1,0:T(8,128)} %bitcast.5, s32[6,256]{1,0:T(8,128)} %bitcast.7, s32[6,1024]{1,0:T(8,128)} %bitcast.6, s32[1,1024]{1,0:T(1,128)} %bitcast.8, s32[1,256]{1,0:T(1,128)} %bitcast.9, ...), custom_call_target="tpu_custom_call" | custom-call | tf_op jit(solution)/shard_map/sweep/pallas_call | solution.py:604
  55.0 0.0 copy-start
  55.0 0.0 copy-start.1
  55.1 2.3 %copy.24 = bf16[1024,512]{1,0:T(8,128)(2,1)} copy(bf16[1024,512]{1,0:T(8,128)(2,1)} %get-tuple-element.6) | data formatting | bytes 2097152
  57.4 0.0 copy-done
  57.4 0.7 %copy.25 = bf16[256,512]{1,0:T(8,128)(2,1)} copy(bf16[256,512]{1,0:T(8,128)(2,1)S(1)} %copy-done) | data formatting | bytes 524288
  58.1 0.0 copy-done.1
  58.1 0.6 %copy.26 = bf16[64,512]{1,0:T(8,128)(2,1)} copy(bf16[64,512]{1,0:T(8,128)(2,1)S(1)} %copy-done.1) | data formatting | bytes 131072
Async XLA Ops:
  55.0 2.3 %copy-start = (bf16[256,512]{1,0:T(8,128)(2,1)S(1)}, bf16[256,512]{1,0:T(8,128)(2,1)}, u32[]{:S(2)}) copy-start(bf16[256,512]{1,0:T(8,128)(2,1)} %get-tuple-element.7) | copy-start | bytes 786436
  55.0 3.0 %copy-start.1 = (bf16[64,512]{1,0:T(8,128)(2,1)S(1)}, bf16[64,512]{1,0:T(8,128)(2,1)}, u32[]{:S(2)}) copy-start(bf16[64,512]{1,0:T(8,128)(2,1)} %get-tuple-element.8) | copy-start | bytes 196612
